TPU v7x, 128 devices: a whole 4x4x4 slice. The times are simulated.
128 devices in a mesh: req: 4 (over x), tp: 32 (over z, y, core).
Axes of the slice: x: 4, y: 4, z: 4, core: 2. Of those that a mesh axis runs over, the one named last changes fastest.
Arguments:
- step_inputs: bfloat16 [4, 256, 1536], P(None, ('req', 'tp')), may hold values from -6 to 6
- qkv_weight: bfloat16 [1536, 2048], replicated, may hold values from -0.15625 to 0.15625
- qkv_bias: float32 [2048], replicated, may hold values from -8 to 8
- out_weight: bfloat16 [1536, 1536], P('tp'), may hold values from -0.15625 to 0.15625
- gate_weight: bfloat16 [1536, 8960], P(None, 'tp'), may hold values from -0.15625 to 0.15625
- up_weight: bfloat16 [1536, 8960], P(None, 'tp'), may hold values from -0.15625 to 0.15625
- down_weight: bfloat16 [8960, 1536], P('tp'), may hold values from -0.0625 to 0.0625
- cache_keys: bfloat16 [256, 4096, 256], P(('req', 'tp')), may hold values from -60 to 60
- cache_values: bfloat16 [256, 4096, 256], P(('req', 'tp')), may hold values from -24 to 24
- lengths: int32 [32, 8], replicated, may hold values from 1 to 4096, as said below
- parents: int32 [4, 32, 8], replicated, may hold values from 0 to 7
- slot_request: int32 [32], replicated, may hold values from 0 to 31, each once
Outputs:
- outputs: bfloat16 [4, 256, 1536], P(None, ('req', 'tp'))
Inputs may be any that keep to these rules, and one draw needn't show every extreme that they name: lengths[r, c] is the number of cached positions of beam c of request r; some beam has exactly 4096. parents[t, r, b] names a beam of the same request r. `slot_request`: a permutation of the requests; slots 8 * i to 8 * i + 7 are rows of index i of req.
All inputs are finite; a program needn't handle non-finite values.
Results may differ from a plain program's by a relative error of at most 0.022.
The roundings to bfloat16 on the way count: a program that leaves them out, or rounds other values in their place, can miss the bound.
Values may be sent and summed in bfloat16 or wider, within the bound.
No kernel may reach another device: no remote copies, remote signals or barrier semaphores. Data moves between devices by JAX's collectives and lax.ppermute only.
A program may use at most 128 MiB of HBM per device.

v0:
```python
import jax
import jax.numpy as jnp
from jax import lax
from jax.sharding import PartitionSpec as P

Q_HEADS = 12
KV_HEADS = 2
theta_base = 1000000.0
norm_eps = 1e-06
masked_score = -1e30


def rms_normed(values):
    values = values.astype(jnp.float32)
    factor = lax.rsqrt(jnp.mean(values * values, axis=-1, keepdims=True) + norm_eps)
    return (values * factor).astype(jnp.bfloat16)


def rotate(vectors, positions):
    half = vectors.shape[-1] // 2
    freqs = theta_base ** (-jnp.arange(half, dtype=jnp.float32) * 2.0 / vectors.shape[-1])
    angles = positions.astype(jnp.float32)[:, None] * freqs[None, :]
    cosine = jnp.cos(angles)[:, None, :]
    sine = jnp.sin(angles)[:, None, :]
    values = vectors.astype(jnp.float32)
    first = values[..., :half]
    second = values[..., half:]
    return jnp.concatenate(
        [first * cosine - second * sine, second * cosine + first * sine], axis=-1
    ).astype(jnp.bfloat16)


def owner_rows(flat, owned_count, beams, inverse):
    owned_global = flat * owned_count + jnp.arange(owned_count, dtype=jnp.int32)
    owned_request = owned_global // beams
    owned_beam = owned_global % beams
    beam_range = jnp.arange(beams, dtype=jnp.int32)
    query_rows = (inverse[owned_request][:, None] * beams + beam_range[None, :]).reshape(-1)
    return (owned_request, owned_beam, query_rows)


def owned_attention(
    every_query, keys, values, owned_request, owned_beam, query_rows, root_all, lengths
):
    owned_rows, context, kv_width = keys.shape
    beams = root_all.shape[1]
    head_dim = kv_width // KV_HEADS
    group = Q_HEADS // KV_HEADS
    grouped = jnp.take(every_query, query_rows, axis=0).reshape(
        owned_rows, beams, KV_HEADS, group, head_dim
    )
    keys = keys.reshape(owned_rows, context, KV_HEADS, head_dim)
    values = values.reshape(owned_rows, context, KV_HEADS, head_dim)
    scores = jnp.einsum(
        "jbkgd,jpkd->jbkgp", grouped, keys, preferred_element_type=jnp.float32
    ) * head_dim ** (-0.5)
    limits = lengths[owned_request, owned_beam]
    live = (jnp.arange(context, dtype=jnp.int32)[None, :] < limits[:, None])[:, None, None, None, :]
    scores = jnp.where(live, scores, masked_score)
    peak = jnp.max(scores, axis=-1)
    weights = jnp.where(live, jnp.exp(scores - peak[..., None]), 0.0)
    total = jnp.sum(weights, axis=-1)
    output = jnp.einsum(
        "jbkgp,jpkd->jbkgd",
        weights.astype(jnp.bfloat16),
        values,
        preferred_element_type=jnp.float32,
    )
    chosen = (root_all[owned_request] == owned_beam[:, None])[:, :, None, None]
    peak = jnp.where(chosen, peak, 0.0).reshape(owned_rows * beams, KV_HEADS, group)
    total = jnp.where(chosen, total, 0.0).reshape(owned_rows * beams, KV_HEADS, group)
    output = jnp.where(chosen[..., None], output, 0.0).reshape(
        owned_rows * beams, KV_HEADS, group, head_dim
    )
    return (peak, total, output)


def spread_rows(pieces, target_rows, row_count):
    return tuple(
        (
            jnp.zeros((row_count,) + piece.shape[1:], jnp.float32).at[target_rows].add(piece)
            for piece in pieces
        )
    )


def per_device(
    step_inputs,
    qkv_weight,
    qkv_bias,
    out_weight,
    gate_weight,
    up_weight,
    down_weight,
    cache_keys,
    cache_values,
    lengths,
    parents,
    slot_request,
):
    steps_count, rows_dev, width = step_inputs.shape
    beams = parents.shape[2]
    requests = slot_request.shape[0]
    req_count = lax.axis_size("req")
    tp_count = lax.axis_size("tp")
    group_requests = requests // req_count
    group_rows = group_requests * beams
    total_rows = requests * beams
    owned_count = cache_keys.shape[0]
    kv_width = cache_keys.shape[2]
    head_dim = kv_width // KV_HEADS
    group = Q_HEADS // KV_HEADS
    attn_width = Q_HEADS * head_dim
    req_index = lax.axis_index("req")
    tp_index = lax.axis_index("tp")
    flat_index = req_index * tp_count + tp_index
    my_requests = lax.dynamic_slice_in_dim(slot_request, req_index * group_requests, group_requests)
    inverse = (
        jnp.zeros((requests,), jnp.int32)
        .at[slot_request]
        .set(jnp.arange(requests, dtype=jnp.int32))
    )
    owned_request, owned_beam, query_rows = owner_rows(flat_index, owned_count, beams, inverse)
    beam_range = jnp.arange(beams, dtype=jnp.int32)
    root_all = jnp.broadcast_to(beam_range[None, :], (requests, beams))
    gen_keys = jnp.zeros((steps_count, group_rows, kv_width), jnp.bfloat16)
    gen_values = jnp.zeros((steps_count, group_rows, kv_width), jnp.bfloat16)
    base_rows = (jnp.arange(group_requests, dtype=jnp.int32) * beams)[:, None]
    column_width = out_weight.shape[0]
    results = []
    for step in range(steps_count):
        root_all = jnp.take_along_axis(root_all, parents[step], axis=1)
        reorder = (base_rows + parents[step][my_requests]).reshape(-1)
        gen_keys = jnp.take(gen_keys, reorder, axis=1)
        gen_values = jnp.take(gen_values, reorder, axis=1)
        inputs = step_inputs[step]
        normed = rms_normed(inputs)
        qkv = (
            jnp.dot(
                lax.all_gather(normed, "tp", axis=0, tiled=True),
                qkv_weight,
                preferred_element_type=jnp.float32,
            )
            + qkv_bias
        ).astype(jnp.bfloat16)
        my_roots = root_all[my_requests]
        positions = (jnp.take_along_axis(lengths[my_requests], my_roots, axis=1) + step).reshape(-1)
        queries = rotate(qkv[:, :attn_width].reshape(group_rows, Q_HEADS, head_dim), positions)
        new_keys = rotate(
            qkv[:, attn_width : attn_width + kv_width].reshape(group_rows, KV_HEADS, head_dim),
            positions,
        )
        gen_keys = gen_keys.at[step].set(new_keys.reshape(group_rows, kv_width))
        gen_values = gen_values.at[step].set(qkv[:, attn_width + kv_width :])
        every_query = lax.all_gather(
            queries.reshape(group_rows, attn_width), "req", axis=0, tiled=True
        )
        part_peak, part_total, part_output = owned_attention(
            every_query,
            cache_keys,
            cache_values,
            owned_request,
            owned_beam,
            query_rows,
            root_all,
            lengths,
        )
        all_peak, all_total, all_output = spread_rows(
            (part_peak, part_total, part_output), query_rows, total_rows
        )
        sum_peak, sum_total, sum_output = lax.psum((all_peak, all_total, all_output), ("req", "tp"))
        peak = lax.dynamic_slice_in_dim(sum_peak, req_index * group_rows, group_rows, 0)
        total = lax.dynamic_slice_in_dim(sum_total, req_index * group_rows, group_rows, 0)
        output = lax.dynamic_slice_in_dim(sum_output, req_index * group_rows, group_rows, 0)
        grouped = queries.reshape(group_rows, KV_HEADS, group, head_dim)
        past_keys = gen_keys[: step + 1].reshape(step + 1, group_rows, KV_HEADS, head_dim)
        past_values = gen_values[: step + 1].reshape(step + 1, group_rows, KV_HEADS, head_dim)
        recent_scores = jnp.einsum(
            "bkgd,sbkd->bkgs", grouped, past_keys, preferred_element_type=jnp.float32
        ) * head_dim ** (-0.5)
        top = jnp.maximum(peak, jnp.max(recent_scores, axis=-1))
        factor = jnp.exp(peak - top)
        recent_weights = jnp.exp(recent_scores - top[..., None])
        denominator = total * factor + jnp.sum(recent_weights, axis=-1)
        numerator = output * factor[..., None] + jnp.einsum(
            "bkgs,sbkd->bkgd",
            recent_weights.astype(jnp.bfloat16),
            past_values,
            preferred_element_type=jnp.float32,
        )
        attention = (
            (numerator / denominator[..., None])
            .reshape(group_rows, attn_width)
            .astype(jnp.bfloat16)
        )
        columns = lax.dynamic_slice_in_dim(attention, tp_index * column_width, column_width, 1)
        attended = lax.psum_scatter(
            jnp.dot(columns, out_weight, preferred_element_type=jnp.float32).astype(jnp.bfloat16),
            "tp",
            scatter_dimension=0,
            tiled=True,
        ).astype(jnp.float32)
        middle = inputs.astype(jnp.float32) + attended
        mixed_in = rms_normed(middle)
        piece = lax.all_gather(mixed_in, "tp", axis=0, tiled=True)
        gate = jnp.dot(piece, gate_weight, preferred_element_type=jnp.float32)
        upward = jnp.dot(piece, up_weight, preferred_element_type=jnp.float32)
        hidden = (jax.nn.silu(gate) * upward).astype(jnp.bfloat16)
        lowered = lax.psum_scatter(
            jnp.dot(hidden, down_weight, preferred_element_type=jnp.float32).astype(jnp.bfloat16),
            "tp",
            scatter_dimension=0,
            tiled=True,
        ).astype(jnp.float32)
        results.append((middle + lowered).astype(jnp.bfloat16))
    return jnp.stack(results)


def solution(mesh):
    in_specs = (
        P(None, ("req", "tp"), None),
        P(),
        P(),
        P("tp", None),
        P(None, "tp"),
        P(None, "tp"),
        P("tp", None),
        P(("req", "tp"), None, None),
        P(("req", "tp"), None, None),
        P(),
        P(),
        P(),
    )
    out_specs = P(None, ("req", "tp"), None)
    return jax.shard_map(
        per_device, mesh=mesh, in_specs=in_specs, out_specs=out_specs, check_vma=False
    )
```

profile of v0, /device:TPU:1, one launch (start us, length us, event | category | flops | bytes accessed | tf_op | source)
XLA Modules:
  0.0 1172.3 jit_solution(9988134711650191990)
XLA Ops:
  28.1 27.6 %all-gather = bf16[32,2,1536]{2,1,0:T(2,128)(2,1)S(1)} all-gather(bf16[1,2,1536]{2,1,0:T(2,128)(2,1)S(1)} %fusion.170), channel_id=1, replica_groups=mesh['req'=4,'tp'=32] {'tp'}, dimensions={0}, use_global_device_ids=true | all-gather | bytes 202752 | tf_op jit(solution)/shard_map/all_gather | solution.py:140
  55.8 4.0 fusion.28
  61.5 12.0 %all_gather.37 = bf16[256,1536]{1,0:T(8,128)(2,1)S(1)} all-gather(bf16[64,1536]{1,0:T(8,128)(2,1)S(1)} %bitcast.314), channel_id=1, replica_groups=mesh['req'=4,'tp'=32] {'req'}, dimensions={0}, use_global_device_ids=true | all-gather | bytes 983040 | tf_op jit(solution)/shard_map/all_gather | solution.py:155
  74.2 7.0 reshape.1079
  81.2 6.9 reshape.1080
  108.8 67.0 %all-reduce.9 = (f32[256,2,6]{0,1,2:T(2,128)S(1)}, f32[256,2,6]{0,1,2:T(2,128)S(1)}) all-reduce(f32[256,2,6]{0,1,2:T(2,128)S(1)} %copy.328, f32[256,2,6]{0,1,2:T(2,128)S(1)} %copy.335), channel_id=1, replica_groups=mesh['req'=4,'tp'=32] {'req','tp'}, use_global_device_ids=true, to_apply=%region_6.10 | all-reduce | flops 6144 | bytes 49152 | tf_op jit(solution)/shard_map/psum | solution.py:171
  185.9 63.2 %all-reduce.20.cloned.1.call-done = f32[256,2,6,128]{3,1,2,0:T(2,128)} async-done(((f32[256,2,6,128]{3,1,2,0:T(2,128)}), f32[256,2,6,128]{3,1,2,0:T(2,128)}) %all-reduce.20.cloned.1.call-update) | async-done | bytes 1572880 | tf_op jit(solution)/shard_map/psum | solution.py:171
  253.4 98.8 %all-reduce.22.cloned.1.call-done = bf16[64,1536]{1,0:T(8,128)(2,1)} async-done(((bf16[64,1536]{1,0:T(8,128)(2,1)}), bf16[64,1536]{1,0:T(8,128)(2,1)}) %all-reduce.22.cloned.1.call-update) | async-done | bytes 196624
  354.6 24.5 %all-gather.4 = bf16[32,2,1536]{2,1,0:T(2,128)(2,1)S(1)} all-gather(bf16[1,2,1536]{2,1,0:T(2,128)(2,1)S(1)} %get-tuple-element.172), channel_id=1, replica_groups=mesh['req'=4,'tp'=32] {'tp'}, dimensions={0}, use_global_device_ids=true | all-gather | bytes 202752 | tf_op jit(solution)/shard_map/all_gather | solution.py:140
  383.8 23.3 %all-gather.2 = bf16[32,2,1536]{2,1,0:T(2,128)(2,1)S(1)} all-gather(bf16[1,2,1536]{2,1,0:T(2,128)(2,1)S(1)} %get-tuple-element.171), channel_id=1, replica_groups=mesh['req'=4,'tp'=32] {'tp'}, dimensions={0}, use_global_device_ids=true | all-gather | bytes 202752 | tf_op jit(solution)/shard_map/all_gather | solution.py:140
  407.2 4.0 fusion.29
  414.6 23.7 %all-gather.6 = bf16[32,2,1536]{2,1,0:T(2,128)(2,1)S(1)} all-gather(bf16[1,2,1536]{2,1,0:T(2,128)(2,1)S(1)} %get-tuple-element.173), channel_id=1, replica_groups=mesh['req'=4,'tp'=32] {'tp'}, dimensions={0}, use_global_device_ids=true | all-gather | bytes 202752 | tf_op jit(solution)/shard_map/all_gather | solution.py:140
  438.5 4.0 fusion.31
  443.4 11.9 %all_gather.46 = bf16[256,1536]{1,0:T(8,128)(2,1)S(1)} all-gather(bf16[64,1536]{1,0:T(8,128)(2,1)S(1)} %bitcast.315), channel_id=1, replica_groups=mesh['req'=4,'tp'=32] {'req'}, dimensions={0}, use_global_device_ids=true | all-gather | bytes 983040 | tf_op jit(solution)/shard_map/all_gather | solution.py:155
  458.1 10.9 all_gather.40
  470.6 11.8 %all_gather.43 = bf16[256,1536]{1,0:T(8,128)(2,1)S(1)} all-gather(bf16[64,1536]{1,0:T(8,128)(2,1)S(1)} %bitcast.317), channel_id=1, replica_groups=mesh['req'=4,'tp'=32] {'req'}, dimensions={0}, use_global_device_ids=true | all-gather | bytes 983040 | tf_op jit(solution)/shard_map/all_gather | solution.py:155
  551.3 30.5 %all-gather.1 = bf16[32,2,1536]{2,1,0:T(2,128)(2,1)S(1)} all-gather(bf16[1,2,1536]{2,1,0:T(2,128)(2,1)S(1)} %copy-done.66), channel_id=1, replica_groups=mesh['req'=4,'tp'=32] {'tp'}, dimensions={0}, use_global_device_ids=true | all-gather | bytes 202752 | tf_op jit(solution)/shard_map/all_gather | solution.py:205
  588.9 119.1 %all-reduce.24.cloned.1.call-done = (f32[256,2,6]{2,1,0:T(2,128)}, f32[256,2,6]{2,1,0:T(2,128)}, f32[256,2,6]{2,1,0:T(2,128)}, f32[256,2,6]{2,1,0:T(2,128)}, f32[256,2,6]{2,1,0:T(2,128)}, /*index=5*/f32[256,2,6]{2,1,0:T(2,128)}) async-done(((f32[256,2,6]{2,1,0:T(2,128)}, f32[256,2,6]{2,1,0:T(2,128)}, f32[256,2,6]{2,1,0:T(2,128)}, f32[256,2,6]{2,1,0:T(2,128)}, f32[256,2,6]{2,1,0:T(2,128)}, ...) | async-done | bytes 73744 | tf_op jit(solution)/shard_map/psum | solution.py:171
  715.0 154.8 %all-reduce.26.cloned.1.call-done = (f32[256,2,6,128]{3,2,1,0:T(8,128)}, f32[256,2,6,128]{3,2,1,0:T(8,128)}, f32[256,2,6,128]{3,2,1,0:T(8,128)}) async-done(((f32[256,2,6,128]{3,2,1,0:T(8,128)}, f32[256,2,6,128]{3,2,1,0:T(8,128)}, f32[256,2,6,128]{3,2,1,0:T(8,128)}), (f32[256,2,6,128]{3,2,1,0:T(8,128)}, f32[256,2,6,128]{3,2,1,0:T(8,128)}, f32[256,2,6,128]{3,2,1,0:T(8,128)})) %all-reduce.26.cloned.1.call-update) | async-done | bytes 4718608 | tf_op jit(solution)/shard_map/psum | solution.py:171
  880.4 100.5 %all-reduce.30.cloned.1.call-done = (bf16[64,1536]{1,0:T(8,128)(2,1)}, bf16[64,1536]{1,0:T(8,128)(2,1)}, bf16[64,1536]{1,0:T(8,128)(2,1)}) async-done(((bf16[64,1536]{1,0:T(8,128)(2,1)}, bf16[64,1536]{1,0:T(8,128)(2,1)}, bf16[64,1536]{1,0:T(8,128)(2,1)}), (bf16[64,1536]{1,0:T(8,128)(2,1)}, bf16[64,1536]{1,0:T(8,128)(2,1)}, bf16[64,1536]{1,0:T(8,128)(2,1)})) %all-reduce.30.cloned.1.call-update) | async-done | bytes 589840
  982.8 24.9 %all-gather.3 = bf16[32,2,1536]{2,1,0:T(2,128)(2,1)S(1)} all-gather(bf16[1,2,1536]{2,1,0:T(2,128)(2,1)S(1)} %get-tuple-element.174), channel_id=1, replica_groups=mesh['req'=4,'tp'=32] {'tp'}, dimensions={0}, use_global_device_ids=true | all-gather | bytes 202752 | tf_op jit(solution)/shard_map/all_gather | solution.py:205
  1009.9 22.5 %all-gather.5 = bf16[32,2,1536]{2,1,0:T(2,128)(2,1)S(1)} all-gather(bf16[1,2,1536]{2,1,0:T(2,128)(2,1)S(1)} %get-tuple-element.176), channel_id=1, replica_groups=mesh['req'=4,'tp'=32] {'tp'}, dimensions={0}, use_global_device_ids=true | all-gather | bytes 202752 | tf_op jit(solution)/shard_map/all_gather | solution.py:205
  1034.5 24.1 %all-gather.7 = bf16[32,2,1536]{2,1,0:T(2,128)(2,1)S(1)} all-gather(bf16[1,2,1536]{2,1,0:T(2,128)(2,1)S(1)} %get-tuple-element.175), channel_id=1, replica_groups=mesh['req'=4,'tp'=32] {'tp'}, dimensions={0}, use_global_device_ids=true | all-gather | bytes 202752 | tf_op jit(solution)/shard_map/all_gather | solution.py:205
  1060.8 102.6 %all-reduce.28.cloned.1.call-done = (bf16[64,1536]{1,0:T(8,128)(2,1)}, bf16[64,1536]{1,0:T(8,128)(2,1)}, bf16[64,1536]{1,0:T(8,128)(2,1)}, bf16[64,1536]{1,0:T(8,128)(2,1)}) async-done(((bf16[64,1536]{1,0:T(8,128)(2,1)}, bf16[64,1536]{1,0:T(8,128)(2,1)}, bf16[64,1536]{1,0:T(8,128)(2,1)}, bf16[64,1536]{1,0:T(8,128)(2,1)}), (bf16[64,1536]{1,0:T(8,128)(2,1)}, bf16[64,1536]{1,0:T(8,128)(2,1)}, ...) | async-done | bytes 786448
  (502 shorter events, 176.0 us)
Async XLA Ops:
  6.5 872.2 %copy-start = (bf16[280,1536]{1,0:T(8,128)(2,1)S(1)}, bf16[280,1536]{1,0:T(8,128)(2,1)}, u32[]{:S(2)}) copy-start(bf16[280,1536]{1,0:T(8,128)(2,1)} %param.42) | copy-start | bytes 2580484
  6.5 242.6 %all-reduce.20.cloned.1.call-start = ((), (), s32[]{:S(2)}) async-start(), calls=%async_computation | async-start | bytes 3145728 | tf_op jit(solution)/shard_map/psum | solution.py:171
  8.8 79.9 %copy-start.68 = (pred[16]{0:T(512)(128)(4,1)}, pred[16]{0:T(512)(128)(4,1)S(1)}, u32[]{:S(2)}) copy-start(pred[16]{0:T(512)(128)(4,1)S(1)} %compare_and_fusion.4) | copy-start | bytes 52
  26.7 29.1 %copy-start.53 = (f32[2048]{0:T(1024)S(1)}, f32[2048]{0:T(1024)}, u32[]{:S(2)}) copy-start(f32[2048]{0:T(1024)} %param.38) | copy-start | bytes 24580
  61.0 20.2 %copy-start.42 = (f32[64,64]{1,0:T(8,128)}, f32[64,64]{1,0:T(8,128)S(1)}, u32[]{:S(2)}) copy-start(f32[64,64]{1,0:T(8,128)S(1)} %get-tuple-element.217) | copy-start | bytes 49156
  61.0 20.2 %copy-start.44 = (f32[64,64]{1,0:T(8,128)}, f32[64,64]{1,0:T(8,128)S(1)}, u32[]{:S(2)}) copy-start(f32[64,64]{1,0:T(8,128)S(1)} %get-tuple-element.218) | copy-start | bytes 49156
  98.5 253.7 %all-reduce.22.cloned.1.call-start = ((), (), s32[]{:S(2)}) async-start(), calls=%async_computation.1 | async-start | bytes 393216
  102.3 78.6 %copy-start.75 = (pred[2,8]{1,0:T(4,128)(4,1)S(1)}, pred[2,8]{1,0:T(4,128)(4,1)}, u32[]{:S(2)}) copy-start(pred[2,8]{1,0:T(4,128)(4,1)} %get-tuple-element.206) | copy-start | bytes 52
  102.3 79.1 %copy-start.73 = (pred[2,8]{1,0:T(4,128)(4,1)S(1)}, pred[2,8]{1,0:T(4,128)(4,1)}, u32[]{:S(2)}) copy-start(pred[2,8]{1,0:T(4,128)(4,1)} %get-tuple-element.208) | copy-start | bytes 52
  102.3 79.7 %copy-start.71 = (pred[2,8]{1,0:T(4,128)(4,1)S(1)}, pred[2,8]{1,0:T(4,128)(4,1)}, u32[]{:S(2)}) copy-start(pred[2,8]{1,0:T(4,128)(4,1)} %get-tuple-element.207) | copy-start | bytes 52
  102.3 80.3 %copy-start.79 = (u32[128]{0:T(128)S(1)}, u32[128]{0:T(128)}, u32[]{:S(2)}) copy-start(u32[128]{0:T(128)} %constant.501) | copy-start | bytes 1540
  107.5 144.8 %copy-start.9 = (bf16[48,1536]{1,0:T(8,128)(2,1)S(1)}, bf16[48,1536]{1,0:T(8,128)(2,1)}, u32[]{:S(2)}) copy-start(bf16[48,1536]{1,0:T(8,128)(2,1)} %param.39) | copy-start | bytes 442372
  253.3 454.6 %all-reduce.24.cloned.1.call-start = ((), (), s32[]{:S(2)}) async-start(), calls=%async_computation.2 | async-start | bytes 3145728 | tf_op jit(solution)/shard_map/psum | solution.py:171
  456.8 26.4 %copy-start.69 = (pred[16]{0:T(512)(128)(4,1)S(1)}, pred[16]{0:T(512)(128)(4,1)}, u32[]{:S(2)}) copy-start(pred[16]{0:T(512)(128)(4,1)} %copy-done.68) | copy-start | bytes 52
  499.4 17.5 %copy-start.55 = (bf16[1,64,256]{2,1,0:T(8,128)(2,1)S(1)}, bf16[1,64,256]{2,1,0:T(8,128)(2,1)}, u32[]{:S(2)}) copy-start(bf16[1,64,256]{2,1,0:T(8,128)(2,1)} %get-tuple-element.151) | copy-start | bytes 98308
  529.2 16.5 %copy-start.62 = (f32[16,2,6]{2,1,0:T(2,128)S(1)}, f32[16,2,6]{2,1,0:T(2,128)}, u32[]{:S(2)}) copy-start(f32[16,2,6]{2,1,0:T(2,128)} %copy.387) | copy-start | bytes 2308
  529.2 17.7 %copy-start.65 = (f32[16,2,6]{2,1,0:T(2,128)S(1)}, f32[16,2,6]{2,1,0:T(2,128)}, u32[]{:S(2)}) copy-start(f32[16,2,6]{2,1,0:T(2,128)} %copy.359) | copy-start | bytes 2308
  529.2 18.9 %copy-start.64 = (f32[16,2,6]{2,1,0:T(2,128)S(1)}, f32[16,2,6]{2,1,0:T(2,128)}, u32[]{:S(2)}) copy-start(f32[16,2,6]{2,1,0:T(2,128)} %copy.345) | copy-start | bytes 2308
  537.9 44.0 %copy-start.52 = (bf16[1,64,256]{2,0,1:T(2,128)(2,1)S(1)}, bf16[1,64,256]{2,0,1:T(2,128)(2,1)}, u32[]{:S(2)}) copy-start(bf16[1,64,256]{2,0,1:T(2,128)(2,1)} %copy.395) | copy-start | bytes 98308
  551.3 318.5 %all-reduce.26.cloned.1.call-start = ((), (), s32[]{:S(2)}) async-start(), calls=%async_computation.3 | async-start | bytes 12582912 | tf_op jit(solution)/shard_map/psum | solution.py:171
  585.8 284.0 %copy-start.29 = (bf16[4,64,256]{2,0,1:T(4,128)(2,1)S(1)}, bf16[4,64,256]{2,0,1:T(4,128)(2,1)}, u32[]{:S(2)}) copy-start(bf16[4,64,256]{2,0,1:T(4,128)(2,1)} %copy-done.28) | copy-start | bytes 393220
  585.8 395.1 %all-reduce.30.cloned.1.call-start = ((), (), s32[]{:S(2)}) async-start(), calls=%async_computation.5 | async-start | bytes 1179648
  587.9 283.4 %copy-start.57 = (f32[64,2,6,2]{2,3,1,0:T(2,128)}, f32[64,2,6,2]{2,3,1,0:T(2,128)S(1)}, u32[]{:S(2)}) copy-start(f32[64,2,6,2]{2,3,1,0:T(2,128)S(1)} %get-tuple-element.230) | copy-start | bytes 18436
  878.3 285.2 %all-reduce.28.cloned.1.call-start = ((), (), s32[]{:S(2)}) async-start(), calls=%async_computation.4 | async-start | bytes 1572864
  (62 other events, 354.3 us)
Sparse Core Ops, SparseCore 0:
  98.6 150.4 all-reduce.19
  253.5 98.6 all-reduce.21
  551.4 156.4 all-reduce.23
  713.0 156.7 all-reduce.25
  878.4 102.5 all-reduce.29
  1060.9 102.4 all-reduce.27
where the time goes:
time: 1180 us; the launch traced here: 1170 us
  waiting for transfers between devices  639 us (54%)
  blocking collectives  315 us (27%)
  local copies, waits for them, and re-layouts  95.5 us (8%)
  other arithmetic  53.3 us (5%)
  matrix products  52.6 us (4%)
  between operations  16.6 us (1%)
    psum x3, waiting for transfers between devices, per_device(): lax.psum((all_peak, all_total, all_output), ('req', 'tp'))  337 us
    unnamed x9, waiting for transfers between devices  302 us
    all_gather x4, blocking collectives, per_device(): piece = lax.all_gather(mixed_in, 'tp', axis=0, tiled=True)  102 us
    all_gather x4, blocking collectives, per_device(): lax.all_gather(normed, 'tp', axis=0, tiled=True)  99.2 us
    psum x1, blocking collectives, per_device(): lax.psum((all_peak, all_total, all_output), ('req', 'tp'))  67 us
    all_gather x4, blocking collectives, per_device(): lax.all_gather(queries.reshape(group_rows, attn_width), 'req', axis=0, ti...  46.6 us
  transfers between devices with their start and end apart: 6, of which 6 were waited for; matrix products, arithmetic and copies ran while one was open for 3% of the time, Pallas kernels for 0%

commit v1 on v0

--- a/solution.py
+++ b/solution.py
@@ -135,9 +135,19 @@
         gen_values = jnp.take(gen_values, reorder, axis=1)
         inputs = step_inputs[step]
         normed = rms_normed(inputs)
+
+        def start_regions(local, axis_tag, dim_at):
+            total_devices = jax.lax.axis_size(axis_tag)
+            rows = tuple((total_devices if to_i == dim_at else 1 for to_i in range(local.ndim)))
+            known = jnp.tile(local, rows)
+            y = jax.lax.all_to_all(
+                known, axis_name=axis_tag, split_axis=dim_at, concat_axis=dim_at, tiled=True
+            )
+            return y
+
         qkv = (
             jnp.dot(
-                lax.all_gather(normed, "tp", axis=0, tiled=True),
+                start_regions(normed, axis_tag="tp", dim_at=0),
                 qkv_weight,
                 preferred_element_type=jnp.float32,
             )

time: 1180 us -> 1150 us (0.975)
  blocking collectives: 315 us -> 214 us
  waiting for transfers between devices: 639 us -> 668 us
  starting transfers between devices: 0.42 us -> 24.8 us
    all_gather x4 -> x0, blocking collectives: 99.2 us -> none  [per_device(): lax.all_gather(normed, 'tp', axis=0, tiled=True)]
    psum x3, waiting for transfers between devices: 337 us -> 363 us  [per_device(): lax.psum((all_peak, all_total, all_output), ('req', 'tp'))]
    all_to_all x0 -> x4, starting transfers between devices: none -> 23.9 us  [start_regions(): jax.lax.all_to_all(known, axis_name=axis_tag, split_axis=dim_at, concat_a...]
  transfers between devices with their start and end apart: 6 -> 10, of which waited for: 6 -> 8; matrix products, arithmetic and copies ran while one was open for 3% -> 9% of each run, Pallas kernels for 0% -> 0%
where the time goes in v1:
time: 1150 us; the launch traced here: 1140 us
  waiting for transfers between devices  668 us (58%)
  blocking collectives  214 us (19%)
  local copies, waits for them, and re-layouts  104 us (9%)
  other arithmetic  63.9 us (6%)
  matrix products  52.6 us (5%)
  starting transfers between devices  24.8 us (2%)
  between operations  16.3 us (1%)
    psum x3, waiting for transfers between devices, per_device(): lax.psum((all_peak, all_total, all_output), ('req', 'tp'))  363 us
    unnamed x9, waiting for transfers between devices  299 us
    all_gather x4, blocking collectives, per_device(): piece = lax.all_gather(mixed_in, 'tp', axis=0, tiled=True)  96.7 us
    psum x1, blocking collectives, per_device(): lax.psum((all_peak, all_total, all_output), ('req', 'tp'))  68.1 us
    all_gather x4, blocking collectives, per_device(): lax.all_gather(queries.reshape(group_rows, attn_width), 'req', axis=0, ti...  48.7 us
    all_to_all x4, starting transfers between devices, start_regions(): jax.lax.all_to_all(known, axis_name=axis_tag, split_axis=dim_at, concat_a...  23.9 us
  transfers between devices with their start and end apart: 10, of which 8 were waited for; matrix products, arithmetic and copies ran while one was open for 9% of the time, Pallas kernels for 0%

profile of v1, /device:TPU:1, one launch (start us, length us, event | category | flops | bytes accessed | tf_op | source)
XLA Modules:
  0.0 1142.7 jit_solution(8045998785299604722)
XLA Ops:
  9.0 9.6 all-to-all-start
  44.5 7.0 reshape.1175
  51.6 6.9 reshape.1176
  65.0 4.0 fusion.28
  70.0 12.0 %all_gather.24 = bf16[256,1536]{1,0:T(8,128)(2,1)S(1)} all-gather(bf16[64,1536]{1,0:T(8,128)(2,1)S(1)} %bitcast.298), channel_id=1, replica_groups=mesh['req'=4,'tp'=32] {'req'}, dimensions={0}, use_global_device_ids=true | all-gather | bytes 983040 | tf_op jit(solution)/shard_map/all_gather | solution.py:165
  98.1 68.1 %all-reduce.9 = (f32[256,2,6]{0,1,2:T(2,128)S(1)}, f32[256,2,6]{0,1,2:T(2,128)S(1)}) all-reduce(f32[256,2,6]{0,1,2:T(2,128)S(1)} %copy.328, f32[256,2,6]{0,1,2:T(2,128)S(1)} %copy.335), channel_id=1, replica_groups=mesh['req'=4,'tp'=32] {'req','tp'}, use_global_device_ids=true, to_apply=%region_6.10 | all-reduce | flops 6144 | bytes 49152 | tf_op jit(solution)/shard_map/psum | solution.py:181
  166.9 77.4 %all-reduce.20.cloned.1.call-done = f32[256,2,6,128]{3,1,2,0:T(2,128)} async-done(((f32[256,2,6,128]{3,1,2,0:T(2,128)}), f32[256,2,6,128]{3,1,2,0:T(2,128)}) %all-reduce.20.cloned.1.call-update) | async-done | bytes 1572880 | tf_op jit(solution)/shard_map/psum | solution.py:181
  251.9 95.5 %all-reduce.22.cloned.1.call-done = bf16[64,1536]{1,0:T(8,128)(2,1)} async-done(((bf16[64,1536]{1,0:T(8,128)(2,1)}), bf16[64,1536]{1,0:T(8,128)(2,1)}) %all-reduce.22.cloned.1.call-update) | async-done | bytes 196624
  349.9 5.5 all-to-all-start.2
  356.3 25.2 %all-gather = bf16[32,2,1536]{2,1,0:T(2,128)(2,1)S(1)} all-gather(bf16[1,2,1536]{2,1,0:T(2,128)(2,1)S(1)} %get-tuple-element.170), channel_id=1, replica_groups=mesh['req'=4,'tp'=32] {'tp'}, dimensions={0}, use_global_device_ids=true | all-gather | bytes 202752 | tf_op jit(solution)/shard_map/all_gather | solution.py:215
  382.4 4.8 all-to-all-start.1
  387.3 4.0 fusion.30
  400.7 4.0 fusion.29
  408.5 4.0 fusion.31
  413.9 12.5 %all_gather.30 = bf16[256,1536]{1,0:T(8,128)(2,1)} all-gather(bf16[64,1536]{1,0:T(8,128)(2,1)S(1)} %bitcast.299), channel_id=1, replica_groups=mesh['req'=4,'tp'=32] {'req'}, dimensions={0}, use_global_device_ids=true | all-gather | bytes 983040 | tf_op jit(solution)/shard_map/all_gather | solution.py:165
  430.2 11.2 all_gather.26
  444.4 13.0 %all_gather.28 = bf16[256,1536]{1,0:T(8,128)(2,1)} all-gather(bf16[64,1536]{1,0:T(8,128)(2,1)S(1)} %bitcast.301), channel_id=1, replica_groups=mesh['req'=4,'tp'=32] {'req'}, dimensions={0}, use_global_device_ids=true | all-gather | bytes 983040 | tf_op jit(solution)/shard_map/all_gather | solution.py:165
  546.6 131.7 %all-reduce.24.cloned.1.call-done = (f32[256,2,6]{2,1,0:T(2,128)}, f32[256,2,6]{2,1,0:T(2,128)}, f32[256,2,6]{2,1,0:T(2,128)}, f32[256,2,6]{2,1,0:T(2,128)}, f32[256,2,6]{2,1,0:T(2,128)}, /*index=5*/f32[256,2,6]{2,1,0:T(2,128)}) async-done(((f32[256,2,6]{2,1,0:T(2,128)}, f32[256,2,6]{2,1,0:T(2,128)}, f32[256,2,6]{2,1,0:T(2,128)}, f32[256,2,6]{2,1,0:T(2,128)}, f32[256,2,6]{2,1,0:T(2,128)}, ...) | async-done | bytes 73744 | tf_op jit(solution)/shard_map/psum | solution.py:181
  686.3 153.9 %all-reduce.26.cloned.1.call-done = (f32[256,2,6,128]{3,2,1,0:T(8,128)}, f32[256,2,6,128]{3,2,1,0:T(8,128)}, f32[256,2,6,128]{3,2,1,0:T(8,128)}) async-done(((f32[256,2,6,128]{3,2,1,0:T(8,128)}, f32[256,2,6,128]{3,2,1,0:T(8,128)}, f32[256,2,6,128]{3,2,1,0:T(8,128)}), (f32[256,2,6,128]{3,2,1,0:T(8,128)}, f32[256,2,6,128]{3,2,1,0:T(8,128)}, f32[256,2,6,128]{3,2,1,0:T(8,128)})) %all-reduce.26.cloned.1.call-update) | async-done | bytes 4718608 | tf_op jit(solution)/shard_map/psum | solution.py:181
  850.8 100.5 %all-reduce.30.cloned.1.call-done = (bf16[64,1536]{1,0:T(8,128)(2,1)}, bf16[64,1536]{1,0:T(8,128)(2,1)}, bf16[64,1536]{1,0:T(8,128)(2,1)}) async-done(((bf16[64,1536]{1,0:T(8,128)(2,1)}, bf16[64,1536]{1,0:T(8,128)(2,1)}, bf16[64,1536]{1,0:T(8,128)(2,1)}), (bf16[64,1536]{1,0:T(8,128)(2,1)}, bf16[64,1536]{1,0:T(8,128)(2,1)}, bf16[64,1536]{1,0:T(8,128)(2,1)})) %all-reduce.30.cloned.1.call-update) | async-done | bytes 589840
  953.2 24.9 %all-gather.1 = bf16[32,2,1536]{2,1,0:T(2,128)(2,1)S(1)} all-gather(bf16[1,2,1536]{2,1,0:T(2,128)(2,1)S(1)} %get-tuple-element.174), channel_id=1, replica_groups=mesh['req'=4,'tp'=32] {'tp'}, dimensions={0}, use_global_device_ids=true | all-gather | bytes 202752 | tf_op jit(solution)/shard_map/all_gather | solution.py:215
  980.2 22.5 %all-gather.2 = bf16[32,2,1536]{2,1,0:T(2,128)(2,1)S(1)} all-gather(bf16[1,2,1536]{2,1,0:T(2,128)(2,1)S(1)} %get-tuple-element.176), channel_id=1, replica_groups=mesh['req'=4,'tp'=32] {'tp'}, dimensions={0}, use_global_device_ids=true | all-gather | bytes 202752 | tf_op jit(solution)/shard_map/all_gather | solution.py:215
  1004.9 24.1 %all-gather.3 = bf16[32,2,1536]{2,1,0:T(2,128)(2,1)S(1)} all-gather(bf16[1,2,1536]{2,1,0:T(2,128)(2,1)S(1)} %get-tuple-element.175), channel_id=1, replica_groups=mesh['req'=4,'tp'=32] {'tp'}, dimensions={0}, use_global_device_ids=true | all-gather | bytes 202752 | tf_op jit(solution)/shard_map/all_gather | solution.py:215
  1031.2 102.6 %all-reduce.28.cloned.1.call-done = (bf16[64,1536]{1,0:T(8,128)(2,1)}, bf16[64,1536]{1,0:T(8,128)(2,1)}, bf16[64,1536]{1,0:T(8,128)(2,1)}, bf16[64,1536]{1,0:T(8,128)(2,1)}) async-done(((bf16[64,1536]{1,0:T(8,128)(2,1)}, bf16[64,1536]{1,0:T(8,128)(2,1)}, bf16[64,1536]{1,0:T(8,128)(2,1)}, bf16[64,1536]{1,0:T(8,128)(2,1)}), (bf16[64,1536]{1,0:T(8,128)(2,1)}, bf16[64,1536]{1,0:T(8,128)(2,1)}, ...) | async-done | bytes 786448
  (473 shorter events, 201.4 us)
Async XLA Ops:
  6.5 842.6 %copy-start = (bf16[280,1536]{1,0:T(8,128)(2,1)S(1)}, bf16[280,1536]{1,0:T(8,128)(2,1)}, u32[]{:S(2)}) copy-start(bf16[280,1536]{1,0:T(8,128)(2,1)} %param.42) | copy-start | bytes 2580484
  9.0 55.9 %all-to-all-start = ((bf16[32,2,1536]{2,1,0:T(2,128)(2,1)}), bf16[32,2,1536]{2,1,0:T(2,128)(2,1)S(1)}, u32[]{:S(2)}, u32[]{:S(2)}) async-start(bf16[32,2,1536]{2,1,0:T(2,128)(2,1)} %tile.8), calls=%async_computation | async-start | bytes 393216 | tf_op jit(solution)/shard_map/all_to_all | solution.py:143
  18.6 225.7 %all-reduce.20.cloned.1.call-start = ((), (), s32[]{:S(2)}) async-start(), calls=%async_computation.4 | async-start | bytes 3145728 | tf_op jit(solution)/shard_map/psum | solution.py:181
  20.9 61.7 %copy-start.50 = (pred[16]{0:T(512)(128)(4,1)}, pred[16]{0:T(512)(128)(4,1)S(1)}, u32[]{:S(2)}) copy-start(pred[16]{0:T(512)(128)(4,1)S(1)} %compare_and_fusion.4) | copy-start | bytes 52
  91.5 255.9 %all-reduce.22.cloned.1.call-start = ((), (), s32[]{:S(2)}) async-start(), calls=%async_computation.5 | async-start | bytes 393216
  92.4 155.1 %copy-start.9 = (bf16[48,1536]{1,0:T(8,128)(2,1)S(1)}, bf16[48,1536]{1,0:T(8,128)(2,1)}, u32[]{:S(2)}) copy-start(bf16[48,1536]{1,0:T(8,128)(2,1)} %param.39) | copy-start | bytes 442372
  95.1 153.6 %copy-start.12 = (bf16[4,64,256]{2,0,1:T(4,128)(2,1)S(1)}, bf16[4,64,256]{2,0,1:T(4,128)(2,1)}, u32[]{:S(2)}) copy-start(bf16[4,64,256]{2,0,1:T(4,128)(2,1)} %copy-done.10) | copy-start | bytes 393220
  95.1 154.5 %copy-start.11 = (bf16[4,64,256]{2,0,1:T(4,128)(2,1)S(1)}, bf16[4,64,256]{2,0,1:T(4,128)(2,1)}, u32[]{:S(2)}) copy-start(bf16[4,64,256]{2,0,1:T(4,128)(2,1)} %copy-done.10) | copy-start | bytes 393220
  95.2 252.2 %copy-start.18 = (bf16[4,2,1536]{2,1,0:T(2,128)(2,1)S(1)}, bf16[4,2,1536]{2,1,0:T(2,128)(2,1)}, u32[]{:S(2)}) copy-start(bf16[4,2,1536]{2,1,0:T(2,128)(2,1)} %param.36) | copy-start | bytes 73732
  96.8 258.7 %copy-start.53 = (pred[64]{0:T(512)(128)(4,1)S(1)}, pred[64]{0:T(512)(128)(4,1)}, u32[]{:S(2)}) copy-start(pred[64]{0:T(512)(128)(4,1)} %get-tuple-element.245) | copy-start | bytes 196
  349.9 31.6 %all-to-all-start.2 = ((bf16[32,2,1536]{2,1,0:T(2,128)(2,1)}), bf16[32,2,1536]{2,1,0:T(2,128)(2,1)S(1)}, u32[]{:S(2)}, u32[]{:S(2)}) async-start(bf16[32,2,1536]{2,1,0:T(2,128)(2,1)} %tile.10), calls=%async_computation.2 | async-start | bytes 393216 | tf_op jit(solution)/shard_map/all_to_all | solution.py:143
  382.4 13.1 %all-to-all-start.1 = ((bf16[32,2,1536]{2,1,0:T(2,128)(2,1)}), bf16[32,2,1536]{2,1,0:T(2,128)(2,1)S(1)}, u32[]{:S(2)}, u32[]{:S(2)}) async-start(bf16[32,2,1536]{2,1,0:T(2,128)(2,1)} %tile.9), calls=%async_computation.1 | async-start | bytes 393216 | tf_op jit(solution)/shard_map/all_to_all | solution.py:143
  396.3 12.2 %all-to-all-start.3 = ((bf16[32,2,1536]{2,1,0:T(2,128)(2,1)}), bf16[32,2,1536]{2,1,0:T(2,128)(2,1)S(1)}, u32[]{:S(2)}, u32[]{:S(2)}) async-start(bf16[32,2,1536]{2,1,0:T(2,128)(2,1)} %tile.11), calls=%async_computation.3 | async-start | bytes 393216 | tf_op jit(solution)/shard_map/all_to_all | solution.py:143
  400.2 278.1 %all-reduce.24.cloned.1.call-start = ((), (), s32[]{:S(2)}) async-start(), calls=%async_computation.6 | async-start | bytes 3145728 | tf_op jit(solution)/shard_map/psum | solution.py:181
  413.8 30.1 %copy-start.32 = (f32[64,64]{1,0:T(8,128)S(1)}, f32[64,64]{1,0:T(8,128)}, u32[]{:S(2)}) copy-start(f32[64,64]{1,0:T(8,128)} %get-tuple-element.182) | copy-start | bytes 49156
  413.8 30.1 %copy-start.34 = (f32[64,64]{1,0:T(8,128)S(1)}, f32[64,64]{1,0:T(8,128)}, u32[]{:S(2)}) copy-start(f32[64,64]{1,0:T(8,128)} %get-tuple-element.183) | copy-start | bytes 49156
  430.1 29.1 %copy-start.51 = (pred[16]{0:T(512)(128)(4,1)S(1)}, pred[16]{0:T(512)(128)(4,1)}, u32[]{:S(2)}) copy-start(pred[16]{0:T(512)(128)(4,1)} %copy-done.50) | copy-start | bytes 52
  478.6 41.0 %copy-start.52 = (pred[64]{0:T(512)(128)(4,1)S(1)}, pred[64]{0:T(512)(128)(4,1)}, u32[]{:S(2)}) copy-start(pred[64]{0:T(512)(128)(4,1)} %get-tuple-element.243) | copy-start | bytes 196
  481.0 22.2 %copy-start.23 = (bf16[4,64,256]{2,0,1:T(4,128)(2,1)}, bf16[4,64,256]{2,0,1:T(4,128)(2,1)S(1)}, u32[]{:S(2)}) copy-start(bf16[4,64,256]{2,0,1:T(4,128)(2,1)S(1)} %scatter.36) | copy-start | bytes 393220
  482.7 38.9 %copy-start.20 = (bf16[4,64,256]{2,0,1:T(4,128)(2,1)}, bf16[4,64,256]{2,0,1:T(4,128)(2,1)S(1)}, u32[]{:S(2)}) copy-start(bf16[4,64,256]{2,0,1:T(4,128)(2,1)S(1)} %scatter.40) | copy-start | bytes 393220
  521.6 318.6 %all-reduce.26.cloned.1.call-start = ((), (), s32[]{:S(2)}) async-start(), calls=%async_computation.7 | async-start | bytes 12582912 | tf_op jit(solution)/shard_map/psum | solution.py:181
  543.7 296.5 %copy-start.26 = (bf16[4,64,256]{2,0,1:T(4,128)(2,1)S(1)}, bf16[4,64,256]{2,0,1:T(4,128)(2,1)}, u32[]{:S(2)}) copy-start(bf16[4,64,256]{2,0,1:T(4,128)(2,1)} %copy-done.25) | copy-start | bytes 393220
  543.7 407.7 %all-reduce.30.cloned.1.call-start = ((), (), s32[]{:S(2)}) async-start(), calls=%async_computation.9 | async-start | bytes 1179648
  848.7 285.2 %all-reduce.28.cloned.1.call-start = ((), (), s32[]{:S(2)}) async-start(), calls=%async_computation.8 | async-start | bytes 1572864
  (48 other events, 276.1 us)
Sparse Core Ops, SparseCore 0:
  91.6 152.6 all-reduce.19
  248.6 98.6 all-reduce.21
  521.7 156.5 all-reduce.23
  683.4 156.7 all-reduce.25
  848.8 102.4 all-reduce.29
  1031.3 102.4 all-reduce.27
